TPU v7x, 32 devices: a whole 2x2x4 slice. The times are simulated.
32 devices in a mesh: comp: 8 (over y, x, core), tile: 4 (over z).
Axes of the slice: x: 2, y: 2, z: 4, core: 2. Of those that a mesh axis runs over, the one named last changes fastest.
Arguments:
- atm_state: float32 [128, 128, 512], P(None, 'comp', 'tile'), may hold values from -6 to 6
- ocean_state: float32 [48, 128, 512], P(None, 'comp', 'tile'), may hold values from -6 to 6
- atm_rate: float32 [128], replicated, may hold values from 0.02 to 0.24
- ocean_rate: float32 [48], replicated, may hold values from 0.02 to 0.24
- ocean_mask: int32 [128, 4], P('comp', 'tile'), may hold values 0 or 1
- remap_weight: bfloat16 [8, 192, 128, 128], P('comp', 'tile'), may hold values from -0.5 to 0.5
- pair_src: int32 [8, 192], P('comp', 'tile'), may hold values from 0 to 63, as said below
- pair_tgt: int32 [8, 192], P('comp', 'tile'), may hold values from 0 to 63, as said below
- pair_count: int32 [8, 4], P('comp', 'tile'), may hold values from 24 to 48, as said below
Outputs:
- atm_next: float32 [128, 128, 512], P(None, 'comp', 'tile')
- ocean_next: float32 [48, 128, 512], P(None, 'comp', 'tile')
Inputs may be any that keep to these rules, and one draw needn't show every extreme that they name: `pair_src`: entry d * 48 + j of row b names atmosphere tile e * 16 + y of band b. Among the first pair_count[b, d] entries of device d at most 13 have the same e, and every device has 13 live entries with one same e. `pair_tgt`: entry d * 48 + j of row b names ocean tile e * 16 + y of band b. Among the first pair_count[b, d] entries of device d at most 13 have the same e, and every device has 13 live entries with one same e. `pair_count`: each row b has some device with 48 live slots.
All inputs are finite; a program needn't handle non-finite values. No bound on the sum of `ocean_mask` on one device may be relied on, other than what follows from the above.
Results may differ from a plain program's by a relative error of at most 0.002.
Values may be sent and summed in bfloat16 or wider, within the bound.
No kernel may reach another device: no remote copies, remote signals or barrier semaphores. Data moves between devices by JAX's collectives and lax.ppermute only.
A program may use at most 64 MiB of HBM per device.

v0:
```python
import jax
import jax.numpy as jnp
from jax import lax
from jax.sharding import PartitionSpec as P

SURF = 8


def padded_2(block, sides, width):
    for axis, dim in sides:
        count = lax.axis_size(axis)
        forward = [(i, i + 1) for i in range(count - 1)]
        forward.append((count - 1, 0))
        backward = [(target, source) for source, target in forward]
        low = lax.ppermute(
            lax.slice_in_dim(block, block.shape[dim] - width, None, axis=dim), axis, forward
        )
        high = lax.ppermute(lax.slice_in_dim(block, 0, width, axis=dim), axis, backward)
        block = jnp.concatenate([low, block, high], axis=dim)
    return block


def relax(padded, spread):
    center = padded[:, 1:-1, 1:-1]
    beside_all = (
        padded[:, 2:, 1:-1] + padded[:, :-2, 1:-1] + padded[:, 1:-1, 2:] + padded[:, 1:-1, :-2]
    )
    return center + spread[:, None, None] * (beside_all - 4.0 * center)


def ghosts(padded, width):
    row_total = padded.shape[1]
    row_index = jnp.arange(row_total)
    position = lax.axis_index("comp")
    at_first = jnp.logical_and(row_index < width, position == 0)
    at_last = jnp.logical_and(row_index >= row_total - width, position == lax.axis_size("comp") - 1)
    retain = jnp.logical_not(jnp.logical_or(at_first, at_last)).astype(jnp.float32)
    return padded * retain[None, :, None]


def shards(
    atm_state,
    ocean_state,
    atm_rate,
    ocean_rate,
    ocean_mask,
    remap_weight,
    pair_src,
    pair_tgt,
    pair_count,
):
    atm_rows = atm_state.shape[1]
    ocean_rows = ocean_state.shape[1]
    cell_total = atm_state.shape[2]
    pair_total = pair_src.shape[1]
    wet_rows = ocean_mask[:, 0].astype(jnp.float32)
    atm_source = atm_state[:SURF].astype(jnp.bfloat16)
    ocean_source = (ocean_state[:SURF] * wet_rows[None, :, None]).astype(jnp.bfloat16)
    atm_band, ocean_band = (
        lax.all_gather(atm_source, "tile", axis=1, tiled=True),
        lax.all_gather(ocean_source, "tile", axis=1, tiled=True),
    )
    anchor = pair_src[0]
    target = pair_tgt[0]
    active = jnp.arange(pair_total) < pair_count[0, 0]
    active_float = active.astype(jnp.float32)[:, None, None]
    weights = remap_weight[0]
    forward = (
        jnp.einsum(
            "fpt,pts->pfs",
            jnp.take(atm_band, anchor, axis=1),
            weights,
            preferred_element_type=jnp.float32,
        )
        * active_float
    )
    reverse = (
        jnp.einsum(
            "fps,pts->pft",
            jnp.take(ocean_band, target, axis=1),
            weights,
            preferred_element_type=jnp.float32,
        )
        * active_float
    )
    band_rows = atm_rows + ocean_rows
    ahead_codes = jnp.where(
        active, target // ocean_rows * band_rows + atm_rows + target % ocean_rows, -1
    )
    back_codes = jnp.where(active, anchor // atm_rows * band_rows + anchor % atm_rows, -1)
    ahead_flat = forward.reshape(pair_total, -1)
    back_flat = reverse.reshape(pair_total, -1)
    row_codes = jnp.arange(band_rows * lax.axis_size("tile"))
    ahead_hot = (row_codes[:, None] == ahead_codes[None, :]).astype(jnp.float32)
    back_hot = (row_codes[:, None] == back_codes[None, :]).astype(jnp.float32)
    summed = lax.psum_scatter(
        jnp.dot(
            ahead_hot,
            ahead_flat,
            precision=lax.Precision.HIGHEST,
            preferred_element_type=jnp.float32,
        )
        + jnp.dot(
            back_hot, back_flat, precision=lax.Precision.HIGHEST, preferred_element_type=jnp.float32
        ),
        "tile",
        scatter_dimension=0,
        tiled=True,
    )
    atm_force = summed[:atm_rows].reshape(atm_rows, SURF, cell_total)
    ocean_force = summed[atm_rows:].reshape(ocean_rows, SURF, cell_total)
    atm_padded = ghosts(padded_2(atm_state, (("comp", 1), ("tile", 2)), 2), 2)
    atm_stepped = relax(ghosts(relax(atm_padded, atm_rate), 1), atm_rate)
    ocean_padded = ghosts(padded_2(ocean_state, (("comp", 1), ("tile", 2)), 2), 2)
    ocean_stepped = relax(ghosts(relax(ocean_padded, ocean_rate), 1), ocean_rate)
    atm_next = atm_stepped.at[:SURF].add(jnp.transpose(atm_force, (1, 0, 2)))
    ocean_next = ocean_stepped.at[:SURF].add(
        jnp.transpose(ocean_force, (1, 0, 2)) * wet_rows[None, :, None]
    )
    return (atm_next, ocean_next)


def solution(mesh):
    return jax.shard_map(
        shards,
        mesh=mesh,
        in_specs=(
            P(None, "comp", "tile"),
            P(None, "comp", "tile"),
            P(),
            P(),
            P("comp", "tile"),
            P("comp", "tile", None, None),
            P("comp", "tile"),
            P("comp", "tile"),
            P("comp", "tile"),
        ),
        out_specs=(P(None, "comp", "tile"), P(None, "comp", "tile")),
        check_vma=False,
    )
```

profile of v0, /device:TPU:0, one launch (start us, length us, event | category | flops | bytes accessed | tf_op | source)
XLA Modules:
  0.0 102.0 jit_solution(3758282511293976926)
XLA Ops:
  7.3 2.0 %copy.67 = f32[128,16,128]{0,1,2:T(8,128)S(1)} copy(f32[128,16,128]{2,1,0:T(8,128)} %param.15) | data formatting | bytes 2097152 | tf_op args[0]
  9.2 0.8 fusion.48
  10.6 2.9 %collective-permute-start.1 = (f32[128,2,128]{0,1,2:T(2,128)}, f32[128,2,128]{0,1,2:T(2,128)}, u32[]{:S(2)}, u32[]{:S(2)}) collective-permute-start(f32[128,2,128]{0,1,2:T(2,128)} %get-tuple-element.38), channel_id=1, source_target_pairs={{4,0},{8,4},{12,8},{16,12},{20,16},{24,20},{28,24},{0,28},{5,1},{9... | collective-permute-start | bytes 393224 | tf_op jit(solution)/shard_map/ppermute | solution.py:18
  13.4 0.8 slice.198
  15.0 14.4 %all_gather.6 = bf16[8,64,128]{2,0,1:T(8,128)(2,1)S(1)} all-gather(bf16[8,16,128]{2,0,1:T(8,128)(2,1)S(1)} %copy.100), channel_id=1, replica_groups=mesh['comp'=8,'tile'=4] {'tile'}, dimensions={1}, use_global_device_ids=true | all-gather | bytes 163840 | tf_op jit(solution)/shard_map/all_gather | solution.py:60
  30.9 14.3 %all_gather.7 = bf16[8,64,128]{2,0,1:T(8,128)(2,1)} all-gather(bf16[8,16,128]{2,0,1:T(8,128)(2,1)S(1)} %fusion.36), channel_id=1, replica_groups=mesh['comp'=8,'tile'=4] {'tile'}, dimensions={1}, use_global_device_ids=true | all-gather | bytes 163840 | tf_op jit(solution)/shard_map/all_gather | solution.py:61
  47.4 2.1 %gather_fusion.1 = bf16[48,8,128]{2,1,0:T(8,128)(2,1)} fusion(bf16[8,64,128]{2,0,1:T(8,128)(2,1)} %all_gather.7, s32[1024]{0:T(1024)S(1)} %pad_clamp_fusion), kind=kCustom, calls=%fused_computation.1.clone | custom fusion | bytes 196800 | tf_op jit(solution)/shard_map/jit(_take)/gather | solution.py:80
  49.6 1.8 %fusion.11 = f32[48,8,128]{2,1,0:T(8,128)S(1)} fusion(bf16[1,48,128,128]{3,2,1,0:T(8,128)(2,1)S(1)} %copy-done, bf16[48,8,128]{2,1,0:T(8,128)(2,1)} %gather_fusion.1, f32[48]{0:T(128)S(1)} %compare_convert_fusion, pred[48]{0:T(512)(128)(4,1)S(1)} %compare_and_fusion), kind=kOutput, calls=%fused_computation.17 | convolution fusion | flops 12681216 | bytes 1868016 | tf_op jit(solution)/shard_map/fps,pts->pft/dot_general | solution.py:78
  51.4 1.9 %convolution_add_fusion = f32[128,1024]{1,0:T(8,128)} fusion(f32[128,1024]{1,0:T(8,128)S(1)} %fusion.26, f32[6,8,8,128]{3,2,1,0:T(8,128)S(1)} %bitcast.52, s32[48]{0:T(128)} %fusion.44), kind=kOutput, calls=%fused_computation.15 | convolution fusion | flops 75634688 | bytes 1245376 | tf_op jit(solution)/shard_map/dot_general | solution.py:103
  53.3 1.4 %fusion.50 = (f32[48,2,128]{2,0,1:T(8,128)}, f32[48,2,128]{2,0,1:T(8,128)S(1)}) fusion(f32[48,16,128]{2,0,1:T(8,128)} %copy-done.2), kind=kLoop, calls=%fused_computation.98 | loop fusion | bytes 196608 | tf_op jit(solution)/shard_map/slice | solution.py:18
  54.8 2.6 %collective-permute-start.5 = (f32[48,2,128]{2,0,1:T(8,128)}, f32[48,2,128]{2,0,1:T(8,128)}, u32[]{:S(2)}, u32[]{:S(2)}) collective-permute-start(f32[48,2,128]{2,0,1:T(8,128)} %get-tuple-element.41), channel_id=1, source_target_pairs={{4,0},{8,4},{12,8},{16,12},{20,16},{24,20},{28,24},{0,28},{5,1},{9... | collective-permute-start | bytes 147464 | tf_op jit(solution)/shard_map/ppermute | solution.py:18
  57.4 1.9 %collective-permute-done.4 = f32[48,2,128]{2,0,1:T(8,128)} collective-permute-done((f32[48,2,128]{2,0,1:T(8,128)S(1)}, f32[48,2,128]{2,0,1:T(8,128)}, u32[]{:S(2)}, u32[]{:S(2)}) %collective-permute-start.4) | collective-permute-done | bytes 49184 | tf_op jit(solution)/shard_map/ppermute | solution.py:15
  61.0 1.1 %fusion.49 = (f32[48,20,2]{2,0,1:T(8,128)}, f32[48,20,2]{2,0,1:T(8,128)}) fusion(f32[48,20,128]{2,0,1:T(8,128)S(1)} %constant_dynamic-update-slice_fusion), kind=kLoop, calls=%fused_computation.97 | loop fusion | bytes 30720 | tf_op jit(solution)/shard_map/slice | solution.py:16
  62.1 1.3 %copy.79 = f32[48,20,2]{0,1,2:T(8,128)S(1)} copy(f32[48,20,2]{2,0,1:T(8,128)} %get-tuple-element.39) | data formatting | bytes 15360 | tf_op jit(solution)/shard_map/slice | solution.py:16
  63.3 1.5 %collective-permute-start.6 = (f32[48,20,2]{0,1,2:T(8,128)S(1)}, f32[48,20,2]{0,1,2:T(8,128)S(1)}, u32[]{:S(2)}, u32[]{:S(2)}) collective-permute-start(f32[48,20,2]{0,1,2:T(8,128)S(1)} %copy.79), channel_id=1, source_target_pairs={{0,1},{1,2},{2,3},{3,0},{4,5},{5,6},{6,7},{7,4},{8,9},{9,10},{10,1... | collective-permute-start | bytes 23048 | tf_op jit(solution)/shard_map/ppermute | solution.py:15
  64.9 1.3 %copy.80 = f32[48,20,2]{0,1,2:T(8,128)S(1)} copy(f32[48,20,2]{2,0,1:T(8,128)} %get-tuple-element.40) | data formatting | bytes 15360 | tf_op jit(solution)/shard_map/slice | solution.py:18
  66.2 2.4 %collective-permute-start.7 = (f32[48,20,2]{0,1,2:T(8,128)S(1)}, f32[48,20,2]{0,1,2:T(8,128)S(1)}, u32[]{:S(2)}, u32[]{:S(2)}) collective-permute-start(f32[48,20,2]{0,1,2:T(8,128)S(1)} %copy.80), channel_id=1, source_target_pairs={{1,0},{2,1},{3,2},{0,3},{5,4},{6,5},{7,6},{4,7},{9,8},{10,9},{11,1... | collective-permute-start | bytes 23048 | tf_op jit(solution)/shard_map/ppermute | solution.py:18
  68.5 0.8 collective-permute-done.6
  69.4 1.0 %copy.81 = f32[48,20,2]{2,0,1:T(8,128)} copy(f32[48,20,2]{0,1,2:T(8,128)S(1)} %collective-permute-done.6) | data formatting | bytes 15360 | tf_op jit(solution)/shard_map/ppermute | solution.py:15
  70.5 1.0 %copy.82 = f32[48,20,2]{2,0,1:T(8,128)} copy(f32[48,20,2]{0,1,2:T(8,128)S(1)} %collective-permute-done.7) | data formatting | bytes 15360 | tf_op jit(solution)/shard_map/ppermute | solution.py:18
  71.5 1.6 %maximum_multiply_fusion.1 = f32[48,20,132]{2,0,1:T(8,128)S(1)} fusion(f32[48,20,2]{2,0,1:T(8,128)} %copy.82, f32[48,20,128]{2,0,1:T(8,128)S(1)} %constant_dynamic-update-slice_fusion, f32[48,20,2]{2,0,1:T(8,128)} %copy.81, f32[20]{0:T(128)S(1)} %not_convert_fusion.1), kind=kLoop, calls=%fused_computation.25 | loop fusion | flops 380160 | bytes 1013840 | tf_op jit(solution)/shard_map/mul | solution.py:38
  73.1 1.0 fusion.20
  74.2 1.2 %pad_maximum_fusion = f32[128,20,128]{0,1,2:T(8,128)S(1)} fusion(f32[128,2,128]{0,1,2:T(2,128)} %collective-permute-done.1, f32[128,16,128]{0,1,2:T(8,128)S(1)} %copy.67, f32[128,2,128]{0,1,2:T(2,128)} %collective-permute-done), kind=kLoop, calls=%fused_computation.2 | loop fusion | flops 655360 | bytes 2621440 | tf_op jit(solution)/shard_map/concatenate | solution.py:19
  75.4 1.3 %collective-permute-start.2 = (f32[128,20,2]{0,1,2:T(8,128)S(1)}, f32[128,20,2]{0,1,2:T(8,128)S(1)}, u32[]{:S(2)}, u32[]{:S(2)}) collective-permute-start(f32[128,20,2]{0,1,2:T(8,128)S(1)} %get-tuple-element.35), channel_id=1, source_target_pairs={{0,1},{1,2},{2,3},{3,0},{4,5},{5,6},{6,7},{7,4},{8,9},{9,10},{10,1... | collective-permute-start | bytes 61448 | tf_op jit(solution)/shard_map/ppermute | solution.py:15
  76.7 3.1 %collective-permute-start.3 = (f32[128,20,2]{0,1,2:T(8,128)S(1)}, f32[128,20,2]{0,1,2:T(8,128)S(1)}, u32[]{:S(2)}, u32[]{:S(2)}) collective-permute-start(f32[128,20,2]{0,1,2:T(8,128)S(1)} %get-tuple-element.36), channel_id=1, source_target_pairs={{1,0},{2,1},{3,2},{0,3},{5,4},{6,5},{7,6},{4,7},{9,8},{10,9},{11,1... | collective-permute-start | bytes 61448 | tf_op jit(solution)/shard_map/ppermute | solution.py:18
  80.5 1.0 collective-permute-done.2
  83.1 0.9 slice_bitcast_fusion
  84.0 1.3 %copy.75 = f32[16,8,128]{1,2,0:T(8,128)} copy(f32[16,8,128]{2,1,0:T(8,128)S(1)} %bitcast.54) | data formatting | bytes 131072 | tf_op jit(solution)/shard_map/reshape | solution.py:110
  85.4 2.3 %slice_add_fusion.3 = f32[8,16,128]{0,2,1:T(8,128)} fusion(f32[128,16,128]{0,2,1:T(8,128)S(1)} %fusion.16, f32[16,8,128]{1,2,0:T(8,128)} %copy.75), kind=kLoop, calls=%fused_computation.18 | loop fusion | flops 16384 | bytes 196608 | tf_op jit(solution)/shard_map/add | solution.py:116
  87.7 5.1 %scatter-add.6 = f32[128,16,128]{0,2,1:T(8,128)S(1)} dynamic-update-slice(f32[128,16,128]{0,2,1:T(8,128)S(1)} %fusion.16, f32[8,16,128]{0,2,1:T(8,128)} %slice_add_fusion.3, s32[]{:T(128)} %constant.113.clone.1, s32[]{:T(128)} %constant.113.clone.1, s32[]{:T(128)} %constant.113.clone.1) | dynamic-update-slice | bytes 131076 | tf_op jit(solution)/shard_map/scatter-add | solution.py:116
  92.8 1.4 %copy.83 = f32[128,16,128]{2,1,0:T(8,128)} copy(f32[128,16,128]{0,2,1:T(8,128)S(1)} %scatter-add.6) | data formatting | bytes 2097152
  94.3 0.9 copy.84
  (60 shorter events, 8.6 us)
Async XLA Ops:
  7.2 39.2 %copy-start = (bf16[1,48,128,128]{3,2,1,0:T(8,128)(2,1)S(1)}, bf16[1,48,128,128]{3,2,1,0:T(8,128)(2,1)}, u32[]{:S(2)}) copy-start(bf16[1,48,128,128]{3,2,1,0:T(8,128)(2,1)} %param.20) | copy-start | bytes 4718596
  7.2 7.1 %copy-start.8 = (s32[1,48]{1,0:T(1,128)S(1)}, s32[1,48]{1,0:T(1,128)}, u32[]{:S(2)}) copy-start(s32[1,48]{1,0:T(1,128)} %param.21) | copy-start | bytes 580
  7.2 7.1 %copy-start.6 = (s32[1,48]{1,0:T(1,128)S(1)}, s32[1,48]{1,0:T(1,128)}, u32[]{:S(2)}) copy-start(s32[1,48]{1,0:T(1,128)} %param.22) | copy-start | bytes 580
  7.2 22.7 %copy-start.1 = (f32[48,16,128]{2,1,0:T(8,128)S(1)}, f32[48,16,128]{2,1,0:T(8,128)}, u32[]{:S(2)}) copy-start(f32[48,16,128]{2,1,0:T(8,128)} %param.16) | copy-start | bytes 1179652
  7.2 22.9 %copy-start.7 = (s32[16,1]{0,1:T(1,128)S(1)}, s32[16,1]{0,1:T(1,128)}, u32[]{:S(2)}) copy-start(s32[16,1]{0,1:T(1,128)} %param.19) | copy-start | bytes 196
  7.2 75.9 %reduce-scatter.2.cloned.1.call-start = ((), (), s32[]{:S(2)}) async-start(), calls=%async_computation.1 | async-start | bytes 655360 | tf_op jit(solution)/shard_map/reduce_scatter | solution.py:96
  10.1 64.1 %collective-permute-start = (f32[128,2,128]{0,1,2:T(2,128)}, f32[128,2,128]{0,1,2:T(2,128)}, u32[]{:S(2)}, u32[]{:S(2)}) collective-permute-start(f32[128,2,128]{0,1,2:T(2,128)} %get-tuple-element.37), channel_id=1, source_target_pairs={{0,4},{4,8},{8,12},{12,16},{16,20},{20,24},{24,28},{28,0},{1,5},{5... | collective-permute-start | bytes 393224 | tf_op jit(solution)/shard_map/ppermute | solution.py:15
  10.6 63.6 %collective-permute-start.1 = (f32[128,2,128]{0,1,2:T(2,128)}, f32[128,2,128]{0,1,2:T(2,128)}, u32[]{:S(2)}, u32[]{:S(2)}) collective-permute-start(f32[128,2,128]{0,1,2:T(2,128)} %get-tuple-element.38), channel_id=1, source_target_pairs={{4,0},{8,4},{12,8},{16,12},{20,16},{24,20},{28,24},{0,28},{5,1},{9... | collective-permute-start | bytes 393224 | tf_op jit(solution)/shard_map/ppermute | solution.py:18
  30.1 0.7 copy-start.2
  46.4 0.6 copy-start.5
  54.8 4.5 %collective-permute-start.4 = (f32[48,2,128]{2,0,1:T(8,128)S(1)}, f32[48,2,128]{2,0,1:T(8,128)}, u32[]{:S(2)}, u32[]{:S(2)}) collective-permute-start(f32[48,2,128]{2,0,1:T(8,128)S(1)} %get-tuple-element.42), channel_id=1, source_target_pairs={{0,4},{4,8},{8,12},{12,16},{16,20},{20,24},{24,28},{28,0},{1,5},{5... | collective-permute-start | bytes 147464 | tf_op jit(solution)/shard_map/ppermute | solution.py:15
  54.8 5.4 %collective-permute-start.5 = (f32[48,2,128]{2,0,1:T(8,128)}, f32[48,2,128]{2,0,1:T(8,128)}, u32[]{:S(2)}, u32[]{:S(2)}) collective-permute-start(f32[48,2,128]{2,0,1:T(8,128)} %get-tuple-element.41), channel_id=1, source_target_pairs={{4,0},{8,4},{12,8},{16,12},{20,16},{24,20},{28,24},{0,28},{5,1},{9... | collective-permute-start | bytes 147464 | tf_op jit(solution)/shard_map/ppermute | solution.py:18
  63.3 6.0 %collective-permute-start.6 = (f32[48,20,2]{0,1,2:T(8,128)S(1)}, f32[48,20,2]{0,1,2:T(8,128)S(1)}, u32[]{:S(2)}, u32[]{:S(2)}) collective-permute-start(f32[48,20,2]{0,1,2:T(8,128)S(1)} %copy.79), channel_id=1, source_target_pairs={{0,1},{1,2},{2,3},{3,0},{4,5},{5,6},{6,7},{7,4},{8,9},{9,10},{10,1... | collective-permute-start | bytes 23048 | tf_op jit(solution)/shard_map/ppermute | solution.py:15
  66.2 4.3 %collective-permute-start.7 = (f32[48,20,2]{0,1,2:T(8,128)S(1)}, f32[48,20,2]{0,1,2:T(8,128)S(1)}, u32[]{:S(2)}, u32[]{:S(2)}) collective-permute-start(f32[48,20,2]{0,1,2:T(8,128)S(1)} %copy.80), channel_id=1, source_target_pairs={{1,0},{2,1},{3,2},{0,3},{5,4},{6,5},{7,6},{4,7},{9,8},{10,9},{11,1... | collective-permute-start | bytes 23048 | tf_op jit(solution)/shard_map/ppermute | solution.py:18
  70.4 2.7 %copy-start.3 = (f32[48]{0:T(128)S(1)}, f32[48]{0:T(128)}, u32[]{:S(2)}) copy-start(f32[48]{0:T(128)} %param.18) | copy-start | bytes 580
  75.4 6.1 %collective-permute-start.2 = (f32[128,20,2]{0,1,2:T(8,128)S(1)}, f32[128,20,2]{0,1,2:T(8,128)S(1)}, u32[]{:S(2)}, u32[]{:S(2)}) collective-permute-start(f32[128,20,2]{0,1,2:T(8,128)S(1)} %get-tuple-element.35), channel_id=1, source_target_pairs={{0,1},{1,2},{2,3},{3,0},{4,5},{5,6},{6,7},{7,4},{8,9},{9,10},{10,1... | collective-permute-start | bytes 61448 | tf_op jit(solution)/shard_map/ppermute | solution.py:15
  76.7 4.9 %collective-permute-start.3 = (f32[128,20,2]{0,1,2:T(8,128)S(1)}, f32[128,20,2]{0,1,2:T(8,128)S(1)}, u32[]{:S(2)}, u32[]{:S(2)}) collective-permute-start(f32[128,20,2]{0,1,2:T(8,128)S(1)} %get-tuple-element.36), channel_id=1, source_target_pairs={{1,0},{2,1},{3,2},{0,3},{5,4},{6,5},{7,6},{4,7},{9,8},{10,9},{11,1... | collective-permute-start | bytes 61448 | tf_op jit(solution)/shard_map/ppermute | solution.py:18
  81.6 0.7 copy-start.4
Sparse Core Ops, SparseCore 0:
  53.4 22.3 reduce-scatter.1
where the time goes:
time: 103 us; the launch traced here: 102 us
  blocking collectives  28.6 us (28%)
  local copies, waits for them, and re-layouts  26.5 us (26%)
  between operations  15 us (15%)
  starting transfers between devices  14.4 us (14%)
  other arithmetic  9.11 us (9%)
  matrix products  4.66 us (5%)
  waiting for transfers between devices  3.77 us (4%)
    all_gather x1, blocking collectives, shards(): lax.all_gather(atm_source, 'tile', axis=1, tiled=True)  14.4 us
    all_gather x1, blocking collectives, shards(): lax.all_gather(ocean_source, 'tile', axis=1, tiled=True)  14.3 us
    ppermute x4, starting transfers between devices, padded_2(): lax.ppermute(lax.slice_in_dim(block, 0, width, axis=dim), axis, backward)  11 us
    unnamed x28, local copies, waits for them, and re-layouts  7.44 us
    scatter-add x1, local copies, waits for them, and re-layouts, shards(): atm_next = atm_stepped.at[:SURF].add(jnp.transpose(atm_force, (1, 0, 2)))  5.1 us
    ppermute x4, waiting for transfers between devices, padded_2(): lax.ppermute(lax.slice_in_dim(block, block.shape[dim] - width, None, axis...  3.67 us
    mul x4, other arithmetic, ghosts(): return padded * retain[None, :, None]  3.33 us
    ppermute x4, starting transfers between devices, padded_2(): lax.ppermute(lax.slice_in_dim(block, block.shape[dim] - width, None, axis...  3.33 us
  transfers between devices with their start and end apart: 9, of which 4 were waited for; matrix products, arithmetic and copies ran while one was open for 24% of the time, Pallas kernels for 0%

commit v1 on v0

--- a/solution.py
+++ b/solution.py
@@ -57,7 +57,9 @@
     atm_source = atm_state[:SURF].astype(jnp.bfloat16)
     ocean_source = (ocean_state[:SURF] * wet_rows[None, :, None]).astype(jnp.bfloat16)
     atm_band, ocean_band = (
-        lax.all_gather(atm_source, "tile", axis=1, tiled=True),
+        jnp.concatenate(
+            lax.all_to_all(jnp.stack([atm_source] * lax.axis_size("tile")), "tile", 0, 0), axis=1
+        ),
         lax.all_gather(ocean_source, "tile", axis=1, tiled=True),
     )
     anchor = pair_src[0]

time: 103 us -> 112 us (1.087)
  blocking collectives: 28.6 us -> 14 us
  waiting for transfers between devices: 3.77 us -> 17.2 us
  starting transfers between devices: 14.4 us -> 19.7 us
  other arithmetic: 9.11 us -> 12.8 us
    reduce_scatter x1, waiting for transfers between devices: 0.02 us -> 16.7 us  [shards(): lax.psum_scatter(jnp.dot(ahead_hot, ahead_flat, precision=lax.Precision.H...]
    all_gather x1 -> x0, blocking collectives: 14.4 us -> none  [shards(): lax.all_gather(atm_source, 'tile', axis=1, tiled=True)]
    all_to_all x0 -> x1, starting transfers between devices: none -> 5.63 us  [shards(): lax.all_to_all(jnp.stack([atm_source] * lax.axis_size('tile')), 'tile', 0...]
    ppermute x4, waiting for transfers between devices: 3.67 us -> 0.49 us  [padded_2(): lax.ppermute(lax.slice_in_dim(block, block.shape[dim] - width, None, axis...]
    gather x1, local copies, waits for them, and re-layouts: 2.15 us -> 0.61 us  [shards(): jnp.take(ocean_band, target, axis=1)]
    unnamed x28 -> x49, local copies, waits for them, and re-layouts: 7.44 us -> 8.48 us
  transfers between devices with their start and end apart: 9 -> 10, of which waited for: 4 -> 2; matrix products, arithmetic and copies ran while one was open for 24% -> 25% of each run, Pallas kernels for 0% -> 0%
where the time goes in v1:
time: 112 us; the launch traced here: 111 us
  local copies, waits for them, and re-layouts  27 us (24%)
  starting transfers between devices  19.7 us (18%)
  waiting for transfers between devices  17.2 us (15%)
  between operations  15.1 us (13%)
  blocking collectives  14 us (12%)
  other arithmetic  12.8 us (11%)
  matrix products  5.02 us (4%)
    reduce_scatter x1, waiting for transfers between devices, shards(): lax.psum_scatter(jnp.dot(ahead_hot, ahead_flat, precision=lax.Precision.H...  16.7 us
    all_gather x1, blocking collectives, shards(): lax.all_gather(ocean_source, 'tile', axis=1, tiled=True)  14 us
    ppermute x4, starting transfers between devices, padded_2(): lax.ppermute(lax.slice_in_dim(block, 0, width, axis=dim), axis, backward)  11.4 us
    unnamed x49, local copies, waits for them, and re-layouts  8.48 us
    all_to_all x1, starting transfers between devices, shards(): lax.all_to_all(jnp.stack([atm_source] * lax.axis_size('tile')), 'tile', 0...  5.63 us
    scatter-add x1, local copies, waits for them, and re-layouts, shards(): atm_next = atm_stepped.at[:SURF].add(jnp.transpose(atm_force, (1, 0, 2)))  5.1 us
    mul x4, other arithmetic, ghosts(): return padded * retain[None, :, None]  3.33 us
    slice x4, local copies, waits for them, and re-layouts, padded_2(): lax.slice_in_dim(block, block.shape[dim] - width, None, axis=dim)  3.13 us
  transfers between devices with their start and end apart: 10, of which 2 were waited for; matrix products, arithmetic and copies ran while one was open for 25% of the time, Pallas kernels for 0%

profile of v1, /device:TPU:0, one launch (start us, length us, event | category | flops | bytes accessed | tf_op | source)
XLA Modules:
  0.0 110.7 jit_solution(16397477024628191455)
XLA Ops:
  7.2 2.0 %copy.69 = f32[128,16,128]{0,1,2:T(8,128)S(1)} copy(f32[128,16,128]{2,1,0:T(8,128)} %param.15) | data formatting | bytes 2097152 | tf_op args[0]
  10.5 2.9 %collective-permute-start.1 = (f32[128,2,128]{0,1,2:T(2,128)}, f32[128,2,128]{0,1,2:T(2,128)}, u32[]{:S(2)}, u32[]{:S(2)}) collective-permute-start(f32[128,2,128]{0,1,2:T(2,128)} %get-tuple-element.38), channel_id=1, source_target_pairs={{4,0},{8,4},{12,8},{16,12},{20,16},{24,20},{28,24},{0,28},{5,1},{9... | collective-permute-start | bytes 393224 | tf_op jit(solution)/shard_map/ppermute | solution.py:18
  14.9 5.6 %all-to-all-start = ((bf16[4,8,16,128]{3,2,1,0:T(8,128)(2,1)}), bf16[4,8,16,128]{3,2,1,0:T(8,128)(2,1)}, u32[]{:S(2)}, u32[]{:S(2)}) async-start(bf16[4,8,16,128]{3,2,1,0:T(8,128)(2,1)} %stack.2), calls=%async_computation | async-start | bytes 262144 | tf_op jit(solution)/shard_map/all_to_all | solution.py:61
  21.3 2.6 %collective-permute-start.5 = (f32[48,2,128]{2,0,1:T(8,128)}, f32[48,2,128]{2,0,1:T(8,128)S(1)}, u32[]{:S(2)}, u32[]{:S(2)}) collective-permute-start(f32[48,2,128]{2,0,1:T(8,128)} %get-tuple-element.41), channel_id=1, source_target_pairs={{4,0},{8,4},{12,8},{16,12},{20,16},{24,20},{28,24},{0,28},{5,1},{9... | collective-permute-start | bytes 147464 | tf_op jit(solution)/shard_map/ppermute | solution.py:18
  25.8 14.0 %all_gather.3 = bf16[8,64,128]{2,0,1:T(8,128)(2,1)S(1)} all-gather(bf16[8,16,128]{2,0,1:T(8,128)(2,1)S(1)} %fusion.36), channel_id=1, replica_groups=mesh['comp'=8,'tile'=4] {'tile'}, dimensions={1}, use_global_device_ids=true | all-gather | bytes 163840 | tf_op jit(solution)/shard_map/all_gather | solution.py:63
  40.4 1.2 %fusion.43 = s32[48]{0:T(128)} fusion(s32[1,48]{1,0:T(1,128)} %param.22, s32[]{:T(128)} %bitcast.52), kind=kLoop, calls=%fused_computation.90 | loop fusion | flops 1152 | bytes 388 | tf_op jit(solution)/shard_map/eq | solution.py:96
  41.5 1.2 %fusion.44 = s32[48]{0:T(128)} fusion(s32[1,48]{1,0:T(1,128)} %param.21, s32[]{:T(128)} %bitcast.54), kind=kLoop, calls=%fused_computation.91 | loop fusion | flops 1104 | bytes 388 | tf_op jit(solution)/shard_map/eq | solution.py:97
  43.3 1.6 %fusion.11 = f32[48,8,128]{2,1,0:T(8,128)} fusion(bf16[1,48,128,128]{3,2,1,0:T(8,128)(2,1)S(1)} %copy-done, bf16[48,8,128]{2,1,0:T(8,128)(2,1)S(1)} %gather_fusion.1, f32[48]{0:T(128)S(1)} %get-tuple-element.46, pred[48]{0:T(512)(128)(4,1)S(1)} %get-tuple-element.45), kind=kOutput, calls=%fused_computation.17 | convolution fusion | flops 12681216 | bytes 1868016 | tf_op jit(solution)/shard_map/fps,pts->pft/dot_general | solution.py:80
  46.5 1.1 fusion.49
  47.6 1.3 %copy.82 = f32[48,20,2]{0,1,2:T(8,128)S(1)} copy(f32[48,20,2]{2,0,1:T(8,128)} %get-tuple-element.39) | data formatting | bytes 15360 | tf_op jit(solution)/shard_map/slice | solution.py:16
  48.9 1.4 %collective-permute-start.6 = (f32[48,20,2]{0,1,2:T(8,128)S(1)}, f32[48,20,2]{0,1,2:T(8,128)S(1)}, u32[]{:S(2)}, u32[]{:S(2)}) collective-permute-start(f32[48,20,2]{0,1,2:T(8,128)S(1)} %copy.82), channel_id=1, source_target_pairs={{0,1},{1,2},{2,3},{3,0},{4,5},{5,6},{6,7},{7,4},{8,9},{9,10},{10,1... | collective-permute-start | bytes 23048 | tf_op jit(solution)/shard_map/ppermute | solution.py:15
  50.3 1.3 %copy.83 = f32[48,20,2]{0,1,2:T(8,128)S(1)} copy(f32[48,20,2]{2,0,1:T(8,128)} %get-tuple-element.40) | data formatting | bytes 15360 | tf_op jit(solution)/shard_map/slice | solution.py:18
  51.5 2.5 %collective-permute-start.7 = (f32[48,20,2]{0,1,2:T(8,128)S(1)}, f32[48,20,2]{0,1,2:T(8,128)S(1)}, u32[]{:S(2)}, u32[]{:S(2)}) collective-permute-start(f32[48,20,2]{0,1,2:T(8,128)S(1)} %copy.83), channel_id=1, source_target_pairs={{1,0},{2,1},{3,2},{0,3},{5,4},{6,5},{7,6},{4,7},{9,8},{10,9},{11,1... | collective-permute-start | bytes 23048 | tf_op jit(solution)/shard_map/ppermute | solution.py:18
  54.5 1.0 copy.84
  55.6 1.0 copy.85
  56.6 1.6 %maximum_multiply_fusion.1 = f32[48,20,132]{2,0,1:T(8,128)S(1)} fusion(f32[48,20,2]{2,0,1:T(8,128)} %copy.85, f32[48,20,128]{2,0,1:T(8,128)S(1)} %constant_dynamic-update-slice_fusion, f32[48,20,2]{2,0,1:T(8,128)} %copy.84, f32[20]{0:T(128)S(1)} %copy-done.14), kind=kLoop, calls=%fused_computation.25 | loop fusion | flops 380160 | bytes 1013840 | tf_op jit(solution)/shard_map/mul | solution.py:38
  58.3 1.0 fusion.20
  59.3 1.2 %pad_maximum_fusion = f32[128,20,128]{0,1,2:T(8,128)S(1)} fusion(f32[128,2,128]{0,1,2:T(2,128)} %collective-permute-done.1, f32[128,16,128]{0,1,2:T(8,128)S(1)} %copy.69, f32[128,2,128]{0,1,2:T(2,128)} %collective-permute-done), kind=kLoop, calls=%fused_computation.2 | loop fusion | flops 655360 | bytes 2621440 | tf_op jit(solution)/shard_map/concatenate | solution.py:19
  60.5 1.2 %copy-done.1 = f32[128,20,128]{0,1,2:T(8,128)} copy-done((f32[128,20,128]{0,1,2:T(8,128)}, f32[128,20,128]{0,1,2:T(8,128)S(1)}, u32[]{:S(2)}) %copy-start.1) | copy-done | bytes 1310744
  62.5 3.4 %collective-permute-start.3 = (f32[128,20,2]{0,1,2:T(8,128)S(1)}, f32[128,20,2]{0,1,2:T(8,128)S(1)}, u32[]{:S(2)}, u32[]{:S(2)}) collective-permute-start(f32[128,20,2]{0,1,2:T(8,128)S(1)} %get-tuple-element.36), channel_id=1, source_target_pairs={{1,0},{2,1},{3,2},{0,3},{5,4},{6,5},{7,6},{4,7},{9,8},{10,9},{11,1... | collective-permute-start | bytes 61448 | tf_op jit(solution)/shard_map/ppermute | solution.py:18
  65.8 0.9 copy.75
  67.7 1.2 %fusion.8 = f32[48,8,128]{2,1,0:T(8,128)S(1)} fusion(bf16[1,48,128,128]{3,2,1,0:T(8,128)(2,1)S(1)} %copy-done, bf16[48,8,128]{2,1,0:T(8,128)(2,1)S(1)} %gather_fusion, f32[48]{0:T(128)} %copy-done.6, pred[48]{0:T(512)(128)(4,1)} %compare_and_fusion.1), kind=kOutput, calls=%fused_computation.16 | convolution fusion | flops 12681216 | bytes 1868016 | tf_op jit(solution)/shard_map/fpt,pts->pfs/dot_general | solution.py:71
  68.9 1.0 fusion.26
  70.0 1.2 %convolution_add_fusion = f32[128,1024]{1,0:T(8,128)} fusion(f32[128,1024]{1,0:T(8,128)S(1)} %fusion.26, f32[6,8,8,128]{3,2,1,0:T(8,128)S(1)} %bitcast.55, s32[48]{0:T(128)S(1)} %copy-done.16), kind=kOutput, calls=%fused_computation.15 | convolution fusion | flops 75634688 | bytes 1245376 | tf_op jit(solution)/shard_map/dot_general | solution.py:105
  71.2 1.2 %fusion.23 = f32[48,16,128]{2,0,1:T(8,128)} fusion(f32[48,18,130]{2,0,1:T(8,128)S(1)} %fusion.20, f32[48]{0:T(128)S(1)} %copy-done.8), kind=kLoop, calls=%fused_computation.36 | loop fusion | flops 688128 | bytes 2359488 | tf_op jit(solution)/shard_map/add | solution.py:28
  75.2 16.7 %reduce-scatter.2.cloned.1.call-done = f32[32,1024]{1,0:T(8,128)} async-done(((f32[128,1024]{1,0:T(8,128)}), f32[32,1024]{1,0:T(8,128)}) %reduce-scatter.2.cloned.1.call-update) | async-done | bytes 131088 | tf_op jit(solution)/shard_map/reduce_scatter | solution.py:98
  91.9 0.9 slice_bitcast_fusion
  92.8 1.3 %copy.78 = f32[16,8,128]{1,2,0:T(8,128)} copy(f32[16,8,128]{2,1,0:T(8,128)S(1)} %bitcast.58) | data formatting | bytes 131072 | tf_op jit(solution)/shard_map/reshape | solution.py:112
  94.1 2.3 %slice_add_fusion.3 = f32[8,16,128]{0,2,1:T(8,128)} fusion(f32[128,16,128]{0,2,1:T(8,128)S(1)} %fusion.16, f32[16,8,128]{1,2,0:T(8,128)} %copy.78), kind=kLoop, calls=%fused_computation.18 | loop fusion | flops 16384 | bytes 196608 | tf_op jit(solution)/shard_map/add | solution.py:118
  96.4 5.1 %scatter-add.6 = f32[128,16,128]{0,2,1:T(8,128)S(1)} dynamic-update-slice(f32[128,16,128]{0,2,1:T(8,128)S(1)} %fusion.16, f32[8,16,128]{0,2,1:T(8,128)} %slice_add_fusion.3, s32[]{:T(128)} %constant.113.clone.1, s32[]{:T(128)} %constant.113.clone.1, s32[]{:T(128)} %constant.113.clone.1) | dynamic-update-slice | bytes 131076 | tf_op jit(solution)/shard_map/scatter-add | solution.py:118
  101.5 1.4 %copy.86 = f32[128,16,128]{2,1,0:T(8,128)} copy(f32[128,16,128]{0,2,1:T(8,128)S(1)} %scatter-add.6) | data formatting | bytes 2097152
  103.0 0.9 copy.87
  (84 shorter events, 12.5 us)
Async XLA Ops:
  7.2 36.2 %copy-start = (bf16[1,48,128,128]{3,2,1,0:T(8,128)(2,1)S(1)}, bf16[1,48,128,128]{3,2,1,0:T(8,128)(2,1)}, u32[]{:S(2)}) copy-start(bf16[1,48,128,128]{3,2,1,0:T(8,128)(2,1)} %param.20) | copy-start | bytes 4718596
  7.2 13.3 %copy-start.4 = (f32[48,16,128]{2,1,0:T(8,128)S(1)}, f32[48,16,128]{2,1,0:T(8,128)}, u32[]{:S(2)}) copy-start(f32[48,16,128]{2,1,0:T(8,128)} %param.16) | copy-start | bytes 1179652
  9.2 14.8 %copy-start.19 = (s32[1,48]{1,0:T(1,128)S(1)}, s32[1,48]{1,0:T(1,128)}, u32[]{:S(2)}) copy-start(s32[1,48]{1,0:T(1,128)} %param.21) | copy-start | bytes 580
  9.2 15.9 %copy-start.17 = (s32[1,48]{1,0:T(1,128)S(1)}, s32[1,48]{1,0:T(1,128)}, u32[]{:S(2)}) copy-start(s32[1,48]{1,0:T(1,128)} %param.22) | copy-start | bytes 580
  9.2 16.0 %copy-start.18 = (s32[16,1]{0,1:T(1,128)S(1)}, s32[16,1]{0,1:T(1,128)}, u32[]{:S(2)}) copy-start(s32[16,1]{0,1:T(1,128)} %param.19) | copy-start | bytes 196
  10.0 49.3 %collective-permute-start = (f32[128,2,128]{0,1,2:T(2,128)}, f32[128,2,128]{0,1,2:T(2,128)}, u32[]{:S(2)}, u32[]{:S(2)}) collective-permute-start(f32[128,2,128]{0,1,2:T(2,128)} %get-tuple-element.37), channel_id=1, source_target_pairs={{0,4},{4,8},{8,12},{12,16},{16,20},{20,24},{24,28},{28,0},{1,5},{5... | collective-permute-start | bytes 393224 | tf_op jit(solution)/shard_map/ppermute | solution.py:15
  10.5 48.8 %collective-permute-start.1 = (f32[128,2,128]{0,1,2:T(2,128)}, f32[128,2,128]{0,1,2:T(2,128)}, u32[]{:S(2)}, u32[]{:S(2)}) collective-permute-start(f32[128,2,128]{0,1,2:T(2,128)} %get-tuple-element.38), channel_id=1, source_target_pairs={{4,0},{8,4},{12,8},{16,12},{20,16},{24,20},{28,24},{0,28},{5,1},{9... | collective-permute-start | bytes 393224 | tf_op jit(solution)/shard_map/ppermute | solution.py:18
  14.9 50.9 %all-to-all-start = ((bf16[4,8,16,128]{3,2,1,0:T(8,128)(2,1)}), bf16[4,8,16,128]{3,2,1,0:T(8,128)(2,1)}, u32[]{:S(2)}, u32[]{:S(2)}) async-start(bf16[4,8,16,128]{3,2,1,0:T(8,128)(2,1)} %stack.2), calls=%async_computation | async-start | bytes 262144 | tf_op jit(solution)/shard_map/all_to_all | solution.py:61
  20.5 71.3 %reduce-scatter.2.cloned.1.call-start = ((), (), s32[]{:S(2)}) async-start(), calls=%async_computation.2 | async-start | bytes 655360 | tf_op jit(solution)/shard_map/reduce_scatter | solution.py:98
  21.3 24.3 %collective-permute-start.4 = (f32[48,2,128]{2,0,1:T(8,128)S(1)}, f32[48,2,128]{2,0,1:T(8,128)}, u32[]{:S(2)}, u32[]{:S(2)}) collective-permute-start(f32[48,2,128]{2,0,1:T(8,128)S(1)} %get-tuple-element.42), channel_id=1, source_target_pairs={{0,4},{4,8},{8,12},{12,16},{16,20},{20,24},{24,28},{28,0},{1,5},{5... | collective-permute-start | bytes 147464 | tf_op jit(solution)/shard_map/ppermute | solution.py:15
  21.3 25.2 %collective-permute-start.5 = (f32[48,2,128]{2,0,1:T(8,128)}, f32[48,2,128]{2,0,1:T(8,128)S(1)}, u32[]{:S(2)}, u32[]{:S(2)}) collective-permute-start(f32[48,2,128]{2,0,1:T(8,128)} %get-tuple-element.41), channel_id=1, source_target_pairs={{4,0},{8,4},{12,8},{16,12},{20,16},{24,20},{28,24},{0,28},{5,1},{9... | collective-permute-start | bytes 147464 | tf_op jit(solution)/shard_map/ppermute | solution.py:18
  25.2 20.4 %copy-start.6 = (f32[48]{0:T(128)}, f32[48]{0:T(128)S(1)}, u32[]{:S(2)}) copy-start(f32[48]{0:T(128)S(1)} %get-tuple-element.46) | copy-start | bytes 580
  25.2 0.6 copy-start.10
  47.6 9.0 %copy-start.14 = (f32[20]{0:T(128)S(1)}, f32[20]{0:T(128)}, u32[]{:S(2)}) copy-start(f32[20]{0:T(128)} %not_convert_fusion.1) | copy-start | bytes 244
  48.9 5.7 %collective-permute-start.6 = (f32[48,20,2]{0,1,2:T(8,128)S(1)}, f32[48,20,2]{0,1,2:T(8,128)S(1)}, u32[]{:S(2)}, u32[]{:S(2)}) collective-permute-start(f32[48,20,2]{0,1,2:T(8,128)S(1)} %copy.82), channel_id=1, source_target_pairs={{0,1},{1,2},{2,3},{3,0},{4,5},{5,6},{6,7},{7,4},{8,9},{9,10},{10,1... | collective-permute-start | bytes 23048 | tf_op jit(solution)/shard_map/ppermute | solution.py:15
  51.5 4.0 %collective-permute-start.7 = (f32[48,20,2]{0,1,2:T(8,128)S(1)}, f32[48,20,2]{0,1,2:T(8,128)S(1)}, u32[]{:S(2)}, u32[]{:S(2)}) collective-permute-start(f32[48,20,2]{0,1,2:T(8,128)S(1)} %copy.83), channel_id=1, source_target_pairs={{1,0},{2,1},{3,2},{0,3},{5,4},{6,5},{7,6},{4,7},{9,8},{10,9},{11,1... | collective-permute-start | bytes 23048 | tf_op jit(solution)/shard_map/ppermute | solution.py:18
  54.1 4.2 %copy-start.12 = (f32[18]{0:T(128)}, f32[18]{0:T(128)S(1)}, u32[]{:S(2)}) copy-start(f32[18]{0:T(128)S(1)} %not_convert_fusion) | copy-start | bytes 220
  55.6 2.7 %copy-start.7 = (f32[48]{0:T(128)S(1)}, f32[48]{0:T(128)}, u32[]{:S(2)}) copy-start(f32[48]{0:T(128)} %param.18) | copy-start | bytes 580
  60.5 1.2 %copy-start.1 = (f32[128,20,128]{0,1,2:T(8,128)}, f32[128,20,128]{0,1,2:T(8,128)S(1)}, u32[]{:S(2)}) copy-start(f32[128,20,128]{0,1,2:T(8,128)S(1)} %pad_maximum_fusion) | copy-start | bytes 3932164
  61.7 11.2 %collective-permute-start.2 = (f32[128,20,2]{0,1,2:T(8,128)S(1)}, f32[128,20,2]{0,1,2:T(8,128)}, u32[]{:S(2)}, u32[]{:S(2)}) collective-permute-start(f32[128,20,2]{0,1,2:T(8,128)S(1)} %get-tuple-element.35), channel_id=1, source_target_pairs={{0,1},{1,2},{2,3},{3,0},{4,5},{5,6},{6,7},{7,4},{8,9},{9,10},{10,1... | collective-permute-start | bytes 61448 | tf_op jit(solution)/shard_map/ppermute | solution.py:15
  62.5 11.2 %collective-permute-start.3 = (f32[128,20,2]{0,1,2:T(8,128)S(1)}, f32[128,20,2]{0,1,2:T(8,128)S(1)}, u32[]{:S(2)}, u32[]{:S(2)}) collective-permute-start(f32[128,20,2]{0,1,2:T(8,128)S(1)} %get-tuple-element.36), channel_id=1, source_target_pairs={{1,0},{2,1},{3,2},{0,3},{5,4},{6,5},{7,6},{4,7},{9,8},{10,9},{11,1... | collective-permute-start | bytes 61448 | tf_op jit(solution)/shard_map/ppermute | solution.py:18
  66.8 3.1 %copy-start.5 = (f32[48,8,128]{2,1,0:T(8,128)S(1)}, f32[48,8,128]{2,1,0:T(8,128)}, u32[]{:S(2)}) copy-start(f32[48,8,128]{2,1,0:T(8,128)} %fusion.11) | copy-start | bytes 589828
  66.9 3.1 %copy-start.16 = (s32[48]{0:T(128)S(1)}, s32[48]{0:T(128)}, u32[]{:S(2)}) copy-start(s32[48]{0:T(128)} %fusion.44) | copy-start | bytes 580
  68.9 2.2 %copy-start.8 = (f32[48]{0:T(128)S(1)}, f32[48]{0:T(128)}, u32[]{:S(2)}) copy-start(f32[48]{0:T(128)} %param.18) | copy-start | bytes 580
  71.2 1.4 %copy-start.2 = (f32[128,20,128]{0,1,2:T(8,128)S(1)}, f32[128,20,128]{0,1,2:T(8,128)}, u32[]{:S(2)}) copy-start(f32[128,20,128]{0,1,2:T(8,128)} %copy-done.1) | copy-start | bytes 3932164
  72.6 1.1 copy-start.15
  73.6 0.7 copy-start.9
  73.6 0.6 copy-start.13
  101.5 1.4 %copy-start.3 = (f32[48,16,128]{2,0,1:T(8,128)S(1)}, f32[48,16,128]{2,0,1:T(8,128)}, u32[]{:S(2)}) copy-start(f32[48,16,128]{2,0,1:T(8,128)} %fusion.23) | copy-start | bytes 1179652
  101.5 1.4 %copy-start.11 = (f32[16]{0:T(128)S(1)}, f32[16]{0:T(128)}, u32[]{:S(2)}) copy-start(f32[16]{0:T(128)} %copy-done.10) | copy-start | bytes 196
Sparse Core Ops, SparseCore 0:
  71.3 20.5 reduce-scatter.1
